TPU v7x, 32 devices: a whole 2x2x4 slice. The times are simulated.
32 devices in a mesh: ctx: 8 (over z, x), chan: 4 (over y, core).
Axes of the slice: x: 2, y: 2, z: 4, core: 2. Of those that a mesh axis runs over, the one named last changes fastest.
Arguments:
- query_in: bfloat16 [4096, 1024], P('chan', 'ctx'), may hold values from -6 to 6
- key_in: bfloat16 [4096, 1024], P('chan', 'ctx'), may hold values from -6 to 6
- value_in: bfloat16 [4096, 1024], P('chan', 'ctx'), may hold values from -6 to 6
- short_kernel: float32 [3, 3, 4096], P(None, None, 'chan'), may hold values from -3.5 to 3.5
- filter_in: float32 [64, 64], replicated, may hold values from -0.75 to 0.75
- filter_out: float32 [64, 4096], P(None, 'chan'), may hold values from -0.75 to 0.75
- filter_decay: float32 [4096], P('chan'), may hold values from 0.5 to 40
- skip_gain: float32 [4096], P('chan'), may hold values from -3 to 3
- grad_out: bfloat16 [4096, 1024], P('chan', 'ctx'), may hold values from -6 to 6
Outputs:
- output: bfloat16 [4096, 1024], P('chan', 'ctx')
- grad_query: bfloat16 [4096, 1024], P('chan', 'ctx')
- grad_key: bfloat16 [4096, 1024], P('chan', 'ctx')
- grad_value: bfloat16 [4096, 1024], P('chan', 'ctx')
- grad_short: float32 [3, 3, 4096], P(None, None, 'chan')
- grad_filter_in: float32 [64, 64], replicated
- grad_filter_out: float32 [64, 4096], P(None, 'chan')
- grad_decay: float32 [4096], P('chan')
- grad_skip: float32 [4096], P('chan')
All inputs are finite; a program needn't handle non-finite values.
Results may differ from a plain program's by a relative error of at most 0.0006.
Values may be sent and summed in bfloat16 or wider, within the bound.
No kernel may reach another device: no remote copies, remote signals or barrier semaphores. Data moves between devices by JAX's collectives and lax.ppermute only.
A program may use at most 128 MiB of HBM per device.

v0:
```python
import math
import jax
import jax.numpy as jnp
from jax import lax
from jax.sharding import PartitionSpec as P

PRECISE = lax.Precision.HIGHEST


def shifted(value, axis, by):
    peers = lax.axis_size(axis)
    pairs = [(i, i + by) for i in range(peers) if 0 <= i + by < peers]
    return lax.ppermute(value, axis, pairs)


def position_features(position, sequence, feature_rows):
    bands = jnp.arange(feature_rows // 2, dtype=jnp.int32)
    factor = 4 * (bands + 1) * (bands + 1)
    phase = position[None, :] * factor[:, None] % sequence
    angles = 2.0 * math.pi / sequence * phase.astype(jnp.float32)
    return jnp.concatenate([jnp.cos(angles), jnp.sin(angles)], axis=0)


def angle_tables(left_index, right_index, modulus):
    phase = left_index[:, None] * right_index[None, :] % modulus
    angles = 2.0 * math.pi / modulus * phase.astype(jnp.float32)
    return (jnp.cos(angles), jnp.sin(angles))


def contract(form, left, right):
    return jnp.einsum(form, left, right, precision=PRECISE)


def times_forward(real_part, imag_part, cosine, sine):
    return (real_part * cosine + imag_part * sine, imag_part * cosine - real_part * sine)


def times_inverse(real_part, imag_part, cosine, sine):
    return (real_part * cosine - imag_part * sine, imag_part * cosine + real_part * sine)


def complex_times(first_real, first_imag, second_real, second_imag):
    return (
        first_real * second_real - first_imag * second_imag,
        first_real * second_imag + first_imag * second_real,
    )


def local_forward(real_part, imag_part):
    length = real_part.shape[-1]
    inner = 64
    outer = length // inner
    leading = real_part.shape[:-1]
    real_part = real_part.reshape(leading + (outer, inner))
    imag_part = imag_part.reshape(leading + (outer, inner))
    outer_index = jnp.arange(outer, dtype=jnp.int32)
    inner_index = jnp.arange(inner, dtype=jnp.int32)
    cos_outer, sin_outer = angle_tables(outer_index, outer_index, outer)
    first_real = contract("cb,...ba->...ca", cos_outer, real_part) + contract(
        "cb,...ba->...ca", sin_outer, imag_part
    )
    first_imag = contract("cb,...ba->...ca", cos_outer, imag_part) - contract(
        "cb,...ba->...ca", sin_outer, real_part
    )
    cos_middle, sin_middle = angle_tables(outer_index, inner_index, length)
    first_real, first_imag = times_forward(first_real, first_imag, cos_middle, sin_middle)
    cos_inner, sin_inner = angle_tables(inner_index, inner_index, inner)
    final_real = contract("...ca,da->...cd", first_real, cos_inner) + contract(
        "...ca,da->...cd", first_imag, sin_inner
    )
    final_imag = contract("...ca,da->...cd", first_imag, cos_inner) - contract(
        "...ca,da->...cd", first_real, sin_inner
    )
    return (final_real, final_imag)


def local_inverse(real_part, imag_part):
    outer = real_part.shape[-2]
    inner = real_part.shape[-1]
    length = outer * inner
    leading = real_part.shape[:-2]
    outer_index = jnp.arange(outer, dtype=jnp.int32)
    inner_index = jnp.arange(inner, dtype=jnp.int32)
    cos_inner, sin_inner = angle_tables(inner_index, inner_index, inner)
    first_real = contract("...cd,ad->...ca", real_part, cos_inner) - contract(
        "...cd,ad->...ca", imag_part, sin_inner
    )
    first_imag = contract("...cd,ad->...ca", imag_part, cos_inner) + contract(
        "...cd,ad->...ca", real_part, sin_inner
    )
    cos_middle, sin_middle = angle_tables(outer_index, inner_index, length)
    first_real, first_imag = times_inverse(first_real, first_imag, cos_middle, sin_middle)
    cos_outer, sin_outer = angle_tables(outer_index, outer_index, outer)
    final_real = contract("bc,...ca->...ba", cos_outer, first_real) - contract(
        "bc,...ca->...ba", sin_outer, first_imag
    )
    final_imag = contract("bc,...ca->...ba", cos_outer, first_imag) + contract(
        "bc,...ca->...ba", sin_outer, first_real
    )
    return (final_real.reshape(leading + (length,)), final_imag.reshape(leading + (length,)))


def held_frequencies(device):
    return 2 * device + jnp.arange(2, dtype=jnp.int32)


def forward_spectrum(signals):
    shards = lax.axis_size("ctx")
    device = lax.axis_index("ctx")
    signal_count, channels, length = signals.shape
    padded = 2 * shards * length
    columns = lax.all_to_all(
        signals.reshape((1, signal_count, channels, length)),
        "ctx",
        split_axis=3,
        concat_axis=0,
        tiled=True,
    )
    shard_index = jnp.arange(shards, dtype=jnp.int32)
    freq_index = jnp.arange(2 * shards, dtype=jnp.int32)
    cos_table, sin_table = angle_tables(freq_index, shard_index, 2 * shards)
    rows_real = contract("qp,pmgb->qmgb", cos_table, columns)
    rows_imag = -contract("qp,pmgb->qmgb", sin_table, columns)
    arrived = lax.all_to_all(
        jnp.stack([rows_real, rows_imag]), "ctx", split_axis=1, concat_axis=4, tiled=True
    )
    spec_real = arrived[0]
    spec_imag = arrived[1]
    freqs = held_frequencies(device)
    cosine, sine = angle_tables(freqs, jnp.arange(length, dtype=jnp.int32), padded)
    spec_real, spec_imag = times_forward(
        spec_real, spec_imag, cosine[:, None, None, :], sine[:, None, None, :]
    )
    return local_forward(spec_real, spec_imag)


def inverse_columns(spec_real, spec_imag):
    shards = lax.axis_size("ctx")
    device = lax.axis_index("ctx")
    real_part, imag_part = local_inverse(spec_real, spec_imag)
    length = real_part.shape[-1]
    padded = 2 * shards * length
    freqs = held_frequencies(device)
    cosine, sine = angle_tables(freqs, jnp.arange(length, dtype=jnp.int32), padded)
    real_part, imag_part = times_inverse(
        real_part, imag_part, cosine[:, None, None, :], sine[:, None, None, :]
    )
    shard_index = jnp.arange(shards, dtype=jnp.int32)
    arrived = lax.all_to_all(
        jnp.stack([real_part, imag_part]), "ctx", split_axis=4, concat_axis=1, tiled=True
    )
    cos_table, sin_table = angle_tables(
        shard_index, jnp.arange(2 * shards, dtype=jnp.int32), 2 * shards
    )
    columns = contract("pq,qmgb->pmgb", cos_table, arrived[0]) - contract(
        "pq,qmgb->pmgb", sin_table, arrived[1]
    )
    return columns * (1.0 / padded)


def to_tokens(columns):
    arrived = lax.all_to_all(columns, "ctx", split_axis=0, concat_axis=3, tiled=True)
    return arrived[0]


def body(
    query_in,
    key_in,
    value_in,
    short_kernel,
    filter_in,
    filter_out,
    filter_decay,
    skip_gain,
    grad_out,
):
    shards = lax.axis_size("ctx")
    device = lax.axis_index("ctx")
    length = query_in.shape[1]
    sequence = shards * length
    scale = sequence ** (-0.5)
    inputs = jnp.stack([query_in, key_in, value_in])
    rim = shifted(inputs[:, :, -2:], "ctx", 1)
    values = inputs.astype(jnp.float32)
    rim_values = rim.astype(jnp.float32)
    before_one = jnp.concatenate([rim_values[..., 1:], values[..., :-1]], axis=-1)
    before_two = jnp.concatenate([rim_values, values[..., :-2]], axis=-1)
    kernel = short_kernel[:, :, :, None]
    shorted = kernel[:, 0] * values + kernel[:, 1] * before_one + kernel[:, 2] * before_two
    query_short = shorted[0]
    key_short = shorted[1]
    value_short = shorted[2]
    gate = key_short * value_short
    position = device * length + jnp.arange(length, dtype=jnp.int32)
    fraction = position.astype(jnp.float32) / sequence
    basis = position_features(position, sequence, filter_in.shape[0])
    preact = jnp.dot(filter_in.T, basis, precision=PRECISE)
    hidden = jnp.sin(preact)
    window = jnp.exp(-filter_decay[:, None] * fraction[None, :])
    taps = window * jnp.dot(filter_out.T, hidden, precision=PRECISE) * scale
    spec_real, spec_imag = forward_spectrum(jnp.stack([gate, taps]))
    gate_real, gate_imag = (spec_real[:, 0], spec_imag[:, 0])
    taps_real, taps_imag = (spec_real[:, 1], spec_imag[:, 1])
    prod_real, prod_imag = complex_times(gate_real, gate_imag, taps_real, taps_imag)
    conv = to_tokens(inverse_columns(prod_real[:, None], prod_imag[:, None]))[0]
    mixed = conv + skip_gain[:, None] * gate
    output = (query_short * mixed).astype(jnp.bfloat16)
    upstream = grad_out.astype(jnp.float32)
    grad_mixed = upstream * query_short
    grad_query_short = upstream * mixed
    upper_real, upper_imag = forward_spectrum(grad_mixed[None])
    upper_real = upper_real[:, 0]
    upper_imag = upper_imag[:, 0]
    along_real, along_imag = complex_times(taps_real, -taps_imag, upper_real, upper_imag)
    cross_real, cross_imag = complex_times(gate_real, -gate_imag, upper_real, upper_imag)
    backward = to_tokens(
        inverse_columns(
            jnp.stack([along_real, cross_real], axis=1), jnp.stack([along_imag, cross_imag], axis=1)
        )
    )
    grad_gate = backward[0] + skip_gain[:, None] * grad_mixed
    grad_taps = backward[1]
    grads = jnp.stack([grad_query_short, grad_gate * value_short, grad_gate * key_short])
    after = shifted(grads[..., :2], "ctx", -1)
    next_one = jnp.concatenate([grads[..., 1:], after[..., :1]], axis=-1)
    next_two = jnp.concatenate([grads[..., 2:], after], axis=-1)
    grad_inputs = (kernel[:, 0] * grads + kernel[:, 1] * next_one + kernel[:, 2] * next_two).astype(
        jnp.bfloat16
    )
    short_terms = jnp.stack(
        [
            jnp.sum(grads * values, axis=-1),
            jnp.sum(grads * before_one, axis=-1),
            jnp.sum(grads * before_two, axis=-1),
        ],
        axis=1,
    )
    weighted = grad_taps * window * scale
    out_terms = jnp.dot(hidden, weighted.T, precision=PRECISE)
    grad_hidden = jnp.dot(filter_out, weighted, precision=PRECISE)
    in_terms = jnp.dot(basis, (grad_hidden * jnp.cos(preact)).T, precision=PRECISE)
    decay_terms = jnp.sum(grad_taps * taps * -fraction[None, :], axis=1)
    skip_terms = jnp.sum(grad_mixed * gate, axis=1)
    short_sum, out_sum, decay_sum, skip_sum = lax.psum(
        (short_terms, out_terms, decay_terms, skip_terms), "ctx"
    )
    in_sum = lax.psum(in_terms, ("ctx", "chan"))
    return (
        output,
        grad_inputs[0],
        grad_inputs[1],
        grad_inputs[2],
        short_sum * scale,
        in_sum * scale,
        out_sum * scale,
        decay_sum * scale,
        skip_sum * scale,
    )


def solution(mesh):
    placed = (
        P("chan", "ctx"),
        P("chan", "ctx"),
        P("chan", "ctx"),
        P(None, None, "chan"),
        P(),
        P(None, "chan"),
        P("chan"),
        P("chan"),
        P("chan", "ctx"),
    )
    return jax.shard_map(
        body,
        mesh=mesh,
        in_specs=placed,
        out_specs=(
            P("chan", "ctx"),
            P("chan", "ctx"),
            P("chan", "ctx"),
            P("chan", "ctx"),
            P(None, None, "chan"),
            P(),
            P(None, "chan"),
            P("chan"),
            P("chan"),
        ),
        check_vma=False,
    )
```

profile of v0, /device:TPU:0, one launch (start us, length us, event | category | flops | bytes accessed | tf_op | source)
XLA Modules:
  0.0 651.2 jit_solution(13803028707653949594)
XLA Ops:
  11.0 4.8 collective-permute-start
  20.5 6.6 %all-to-all-start.4 = ((f32[1,1,1024,128]{2,1,0,3:T(1,128)}), f32[1,1,1024,128]{2,1,0,3:T(1,128)}, u32[]{:S(2)}, u32[]{:S(2)}) async-start(f32[1,1,1024,128]{2,1,0,3:T(1,128)} %copy.246), calls=%async_computation.4 | async-start | bytes 1048576 | tf_op jit(solution)/shard_map/all_to_all | solution.py:112
  32.8 7.8 %all-to-all-done.4 = f32[1,1,1024,128]{2,1,0,3:T(1,128)} async-done(((f32[1,1,1024,128]{2,1,0,3:T(1,128)}), f32[1,1,1024,128]{2,1,0,3:T(1,128)}, u32[]{:S(2)}, u32[]{:S(2)}) %all-to-all-start.4) | async-done | bytes 524320 | tf_op jit(solution)/shard_map/all_to_all | solution.py:112
  51.2 18.4 %all-to-all-done = f32[1,2,1024,128]{2,1,0,3:T(2,128)} async-done(((f32[1,2,1024,128]{2,1,0,3:T(2,128)}), f32[1,2,1024,128]{2,1,0,3:T(2,128)}, u32[]{:S(2)}, u32[]{:S(2)}) %all-to-all-start) | async-done | bytes 1048608 | tf_op jit(solution)/shard_map/all_to_all | solution.py:112
  86.3 35.7 %all-to-all-done.5 = f32[2,16,1,1024,16]{3,4,2,0,1:T(8,128)} async-done(((f32[2,16,1,1024,16]{3,4,2,0,1:T(8,128)}), f32[2,16,1,1024,16]{3,4,2,0,1:T(8,128)}, u32[]{:S(2)}, u32[]{:S(2)}) %all-to-all-start.5) | async-done | bytes 2097184 | tf_op jit(solution)/shard_map/all_to_all | solution.py:124
  145.3 5.7 subtract_bitcast_fusion.1
  157.5 61.7 %all-to-all-done.1 = f32[2,16,2,1024,16]{3,4,2,0,1:T(8,128)} async-done(((f32[2,16,2,1024,16]{3,4,2,0,1:T(8,128)}), f32[2,16,2,1024,16]{3,4,2,0,1:T(8,128)}, u32[]{:S(2)}, u32[]{:S(2)}) %all-to-all-start.1) | async-done | bytes 4194336 | tf_op jit(solution)/shard_map/all_to_all | solution.py:124
  224.1 7.9 %fusion.26 = f32[2,2,1024,64,2]{2,4,3,1,0:T(2,128)S(1)} fusion(f32[2,2,1024,2,64]{2,4,3,1,0:T(8,128)S(1)} %get-tuple-element.68), kind=kOutput, calls=%fused_computation.48 | convolution fusion | flops 12582968 | bytes 4194304 | tf_op jit(solution)/shard_map/cb,...ba->...ca/dot_general | solution.py:31
  232.0 8.3 %fusion.22 = f32[2,2,1024,64,2]{2,4,3,1,0:T(2,128)S(1)} fusion(f32[2,2,1024,2,64]{2,4,3,1,0:T(8,128)S(1)} %get-tuple-element.69), kind=kOutput, calls=%fused_computation.44 | convolution fusion | flops 12582968 | bytes 4194304 | tf_op jit(solution)/shard_map/cb,...ba->...ca/dot_general | solution.py:31
  240.3 8.2 %convolution_add_fusion = f32[2,2,1024,64,2]{2,4,3,1,0:T(2,128)S(1)} fusion(f32[2,2,1024,64,2]{2,4,3,1,0:T(2,128)S(1)} %fusion.26, f32[2,2,1024,2,64]{2,4,3,1,0:T(8,128)S(1)} %get-tuple-element.69), kind=kOutput, calls=%fused_computation.42 | convolution fusion | flops 13107256 | bytes 6291456 | tf_op jit(solution)/shard_map/cb,...ba->...ca/dot_general | solution.py:31
  248.6 11.2 %fusion.2 = (f32[2,2,1024,2,64]{2,3,4,1,0:T(2,128)S(1)}, f32[2,2,1024,2,64]{2,3,4,1,0:T(2,128)S(1)}) fusion(f32[2,2,1024,64,2]{2,4,3,1,0:T(2,128)S(1)} %convolution_add_fusion, f32[2,64]{0,1:T(8,128)S(1)} %copy-done.21, f32[2,64]{0,1:T(8,128)S(1)} %copy-done.23, f32[2,2,1024,64,2]{2,4,3,1,0:T(2,128)S(1)} %fusion.22, ...), kind=kOutput, calls=%fused_computation.14 | convolution fusion | flops 16252984 | bytes 10486784 | tf_op jit(solution)/shard_map/cb,...ba->...ca/dot_general | solution.py:31
  284.9 9.6 %multiply_subtract_fusion = (f32[2,2,1024,2,64]{2,3,4,1,0:T(2,128)S(1)}, f32[2,2,1024,2,64]{2,3,4,1,0:T(2,128)S(1)}) fusion(f32[2,64]{0,1:T(8,128)S(1)} %copy-done.21, f32[2,64]{0,1:T(8,128)S(1)} %copy-done.23, f32[2,2,1024,2,64]{2,4,3,1,0:T(8,128)S(1)} %fusion.13, f32[2,2,1024,2,64]{2,4,3,1,0:T(8,128)S(1)} %fusion.15, ...), kind=kLoop, calls=%fused_computation.23 | loop fusion | flops 4194304 | bytes 12583936 | tf_op jit(solution)/shard_map/sub | solution.py:39
  294.5 7.5 %fusion.190 = f32[2,2,1024,64,2]{2,4,3,1,0:T(2,128)S(1)} fusion(f32[2,2,1024,2,64]{2,3,4,1,0:T(2,128)S(1)} %get-tuple-element.60), kind=kOutput, calls=%fused_computation.283 | convolution fusion | flops 12582968 | bytes 4194304 | tf_op jit(solution)/shard_map/bc,...ca->...ba/dot_general | solution.py:31
  302.0 7.5 %fusion.188 = f32[2,2,1024,64,2]{2,4,3,1,0:T(2,128)S(1)} fusion(f32[2,2,1024,2,64]{2,3,4,1,0:T(2,128)S(1)} %get-tuple-element.61), kind=kOutput, calls=%fused_computation.281 | convolution fusion | flops 12582968 | bytes 4194304 | tf_op jit(solution)/shard_map/bc,...ca->...ba/dot_general | solution.py:31
  309.6 8.4 %subtract_bitcast_fusion = f32[2,2,1024,2,64]{2,3,4,1,0:T(2,128)S(1)} fusion(f32[2,2,1024,64,2]{2,4,3,1,0:T(2,128)S(1)} %fusion.190, f32[2,2,1024,2,64]{2,3,4,1,0:T(2,128)S(1)} %get-tuple-element.61), kind=kOutput, calls=%fused_computation.21 | convolution fusion | flops 13107256 | bytes 6291456 | tf_op jit(solution)/shard_map/bc,...ca->...ba/dot_general | solution.py:31
  317.9 8.0 %add_bitcast_fusion = f32[2,2,1024,2,64]{2,3,4,1,0:T(2,128)S(1)} fusion(f32[2,2,1024,64,2]{2,4,3,1,0:T(2,128)S(1)} %fusion.188, f32[2,2,1024,2,64]{2,3,4,1,0:T(2,128)S(1)} %get-tuple-element.60), kind=kOutput, calls=%fused_computation.20 | convolution fusion | flops 13107256 | bytes 6291456 | tf_op jit(solution)/shard_map/bc,...ca->...ba/dot_general | solution.py:31
  328.8 5.2 copy.268
  334.0 5.0 all-to-all-start.6
  366.8 64.8 %all-to-all-done.6 = f32[2,2,2,1024,128]{3,2,1,0,4:T(2,128)} async-done(((f32[2,2,2,1024,128]{3,2,1,0,4:T(2,128)}), f32[2,2,2,1024,128]{3,2,1,0,4:T(2,128)}, u32[]{:S(2)}, u32[]{:S(2)}) %all-to-all-start.6) | async-done | bytes 4194336 | tf_op jit(solution)/shard_map/all_to_all | solution.py:149
  462.9 20.8 %all-to-all-done.2 = f32[2,2,1,1024,128]{3,1,2,0,4:T(2,128)} async-done(((f32[2,2,1,1024,128]{3,1,2,0,4:T(2,128)}), f32[2,2,1,1024,128]{3,1,2,0,4:T(2,128)}, u32[]{:S(2)}, u32[]{:S(2)}) %all-to-all-start.2) | async-done | bytes 2097184 | tf_op jit(solution)/shard_map/all_to_all | solution.py:149
  506.5 7.3 %all-to-all-done.7 = f32[8,2,1024,16]{2,3,1,0:T(8,128)} async-done(((f32[8,2,1024,16]{2,3,1,0:T(8,128)}), f32[8,2,1024,16]{2,3,1,0:T(8,128)}, u32[]{:S(2)}, u32[]{:S(2)}) %all-to-all-start.7) | async-done | bytes 1048608 | tf_op jit(solution)/shard_map/all_to_all | solution.py:162
  523.4 40.9 %psum.36 = f32[64,64]{1,0:T(8,128)S(1)} all-reduce(f32[64,64]{1,0:T(8,128)} %fusion.105), channel_id=1, replica_groups=mesh['ctx'=8,'chan'=4] {'ctx','chan'}, use_global_device_ids=true, to_apply=%region_4.5 | all-reduce | flops 4096 | bytes 32768 | tf_op jit(solution)/shard_map/psum | solution.py:247
  574.1 37.3 %all-reduce = (f32[3,3,1024]{2,0,1:T(4,128)S(1)}, f32[1024]{0:T(1024)S(1)}, f32[1024]{0:T(1024)S(1)}) all-reduce(f32[3,3,1024]{2,0,1:T(4,128)S(1)} %pad_maximum_fusion.14, f32[1024]{0:T(1024)S(1)} %get-tuple-element.106, f32[1024]{0:T(1024)S(1)} %get-tuple-element.96), channel_id=1, replica_groups=mesh['ctx'=8,'chan'=4] {'ctx'}, use_global_device_ids=true, to_apply=%region_3.4 | all-reduce | flops 11264 | bytes 90112 | tf_op jit(solution)/shard_map/psum | solution.py:244
  621.0 21.3 %all-reduce.3.cloned.1.call-done = f32[64,1024]{1,0:T(8,128)} async-done(((f32[64,1024]{1,0:T(8,128)}), f32[64,1024]{1,0:T(8,128)}) %all-reduce.3.cloned.1.call-update) | async-done | bytes 262160 | tf_op jit(solution)/shard_map/psum | solution.py:244
  (212 shorter events, 215.7 us)
Async XLA Ops:
  7.2 22.2 %copy-start = (f32[64,1024]{1,0:T(8,128)S(1)}, f32[64,1024]{1,0:T(8,128)}, u32[]{:S(2)}) copy-start(f32[64,1024]{1,0:T(8,128)} %param.14) | copy-start | bytes 786436
  8.3 7.5 %copy-start.27 = (f32[3,3,1024]{2,1,0:T(4,128)S(1)}, f32[3,3,1024]{2,1,0:T(4,128)}, u32[]{:S(2)}) copy-start(f32[3,3,1024]{2,1,0:T(4,128)} %param.12) | copy-start | bytes 110596
  8.3 7.7 %copy-start.36 = (f32[1024]{0:T(1024)S(1)}, f32[1024]{0:T(1024)}, u32[]{:S(2)}) copy-start(f32[1024]{0:T(1024)} %param.15) | copy-start | bytes 12292
  8.4 7.8 %copy-start.19 = (bf16[1024,128]{1,0:T(8,128)(2,1)S(1)}, bf16[1024,128]{1,0:T(8,128)(2,1)}, u32[]{:S(2)}) copy-start(bf16[1024,128]{1,0:T(8,128)(2,1)} %param.17) | copy-start | bytes 786436
  9.6 7.4 %copy-start.11 = (bf16[1024,128]{0,1:T(8,128)(2,1)}, bf16[1024,128]{0,1:T(8,128)(2,1)S(1)}, u32[]{:S(2)}) copy-start(bf16[1024,128]{0,1:T(8,128)(2,1)S(1)} %copy.215) | copy-start | bytes 786436
  10.8 6.5 copy-start.12
  11.0 6.2 collective-permute-start
  20.5 20.0 %all-to-all-start.4 = ((f32[1,1,1024,128]{2,1,0,3:T(1,128)}), f32[1,1,1024,128]{2,1,0,3:T(1,128)}, u32[]{:S(2)}, u32[]{:S(2)}) async-start(f32[1,1,1024,128]{2,1,0,3:T(1,128)} %copy.246), calls=%async_computation.4 | async-start | bytes 1048576 | tf_op jit(solution)/shard_map/all_to_all | solution.py:112
  40.6 29.0 %all-to-all-start = ((f32[1,2,1024,128]{2,1,0,3:T(2,128)}), f32[1,2,1024,128]{2,1,0,3:T(2,128)}, u32[]{:S(2)}, u32[]{:S(2)}) async-start(f32[1,2,1024,128]{2,1,0,3:T(2,128)} %copy.217), calls=%async_computation | async-start | bytes 2097152 | tf_op jit(solution)/shard_map/all_to_all | solution.py:112
  69.6 52.4 %all-to-all-start.5 = ((f32[2,16,1,1024,16]{3,4,2,0,1:T(8,128)}), f32[2,16,1,1024,16]{3,4,2,0,1:T(8,128)}, u32[]{:S(2)}, u32[]{:S(2)}) async-start(f32[2,16,1,1024,16]{3,4,2,0,1:T(8,128)} %copy.248), calls=%async_computation.5 | async-start | bytes 4194304 | tf_op jit(solution)/shard_map/all_to_all | solution.py:124
  122.0 97.3 %all-to-all-start.1 = ((f32[2,16,2,1024,16]{3,4,2,0,1:T(8,128)}), f32[2,16,2,1024,16]{3,4,2,0,1:T(8,128)}, u32[]{:S(2)}, u32[]{:S(2)}) async-start(f32[2,16,2,1024,16]{3,4,2,0,1:T(8,128)} %copy.220), calls=%async_computation.1 | async-start | bytes 8388608 | tf_op jit(solution)/shard_map/all_to_all | solution.py:124
  141.2 4.1 copy-start.20
  141.2 4.1 copy-start.22
  151.1 4.0 copy-start.15
  240.3 8.3 %copy-start.21 = (f32[2,64]{0,1:T(8,128)S(1)}, f32[2,64]{0,1:T(8,128)}, u32[]{:S(2)}) copy-start(f32[2,64]{0,1:T(8,128)} %copy.229) | copy-start | bytes 1540
  240.3 8.3 %copy-start.23 = (f32[2,64]{0,1:T(8,128)S(1)}, f32[2,64]{0,1:T(8,128)}, u32[]{:S(2)}) copy-start(f32[2,64]{0,1:T(8,128)} %copy.226) | copy-start | bytes 1540
  334.0 97.5 %all-to-all-start.6 = ((f32[2,2,2,1024,128]{3,2,1,0,4:T(2,128)}), f32[2,2,2,1024,128]{3,2,1,0,4:T(2,128)}, u32[]{:S(2)}, u32[]{:S(2)}) async-start(f32[2,2,2,1024,128]{3,2,1,0,4:T(2,128)} %copy.268), calls=%async_computation.6 | async-start | bytes 8388608 | tf_op jit(solution)/shard_map/all_to_all | solution.py:149
  358.5 4.7 copy-start.35
  431.5 52.2 %all-to-all-start.2 = ((f32[2,2,1,1024,128]{3,1,2,0,4:T(2,128)}), f32[2,2,1,1024,128]{3,1,2,0,4:T(2,128)}, u32[]{:S(2)}, u32[]{:S(2)}) async-start(f32[2,2,1,1024,128]{3,1,2,0,4:T(2,128)} %copy.240), calls=%async_computation.2 | async-start | bytes 4194304 | tf_op jit(solution)/shard_map/all_to_all | solution.py:149
  483.7 30.1 %all-to-all-start.7 = ((f32[8,2,1024,16]{2,3,1,0:T(8,128)}), f32[8,2,1024,16]{2,3,1,0:T(8,128)}, u32[]{:S(2)}, u32[]{:S(2)}) async-start(f32[8,2,1024,16]{2,3,1,0:T(8,128)} %copy.272), calls=%async_computation.7 | async-start | bytes 2097152 | tf_op jit(solution)/shard_map/all_to_all | solution.py:162
  513.8 53.3 %all-to-all-start.3 = ((f32[8,1,1024,16]{2,3,1,0:T(8,128)}), f32[8,1,1024,16]{2,3,1,0:T(8,128)}, u32[]{:S(2)}, u32[]{:S(2)}) async-start(f32[8,1,1024,16]{2,3,1,0:T(8,128)} %copy.244), calls=%async_computation.3 | async-start | bytes 1048576 | tf_op jit(solution)/shard_map/all_to_all | solution.py:162
  517.9 124.3 %all-reduce.3.cloned.1.call-start = ((), (), s32[]{:S(2)}) async-start(), calls=%async_computation.8 | async-start | bytes 524288 | tf_op jit(solution)/shard_map/psum | solution.py:244
  567.0 4.7 copy-start.26
  612.0 5.7 collective-permute-start.1
  (25 other events, 56.2 us)
Sparse Core Ops, SparseCore 0:
  571.8 70.4 all-reduce.2
where the time goes:
time: 659 us; the launch traced here: 651 us
  waiting for transfers between devices  241 us (37%)
  matrix products  162 us (25%)
  local copies, waits for them, and re-layouts  82.3 us (12%)
  blocking collectives  78.2 us (12%)
  starting transfers between devices  44.5 us (7%)
  other arithmetic  28.1 us (4%)
  between operations  15.7 us (2%)
    dot_general x40, matrix products, contract(): return jnp.einsum(form, left, right, precision=PRECISE)  156 us
    all_to_all x2, waiting for transfers between devices, forward_spectrum(): lax.all_to_all(jnp.stack([rows_real, rows_imag]), 'ctx', split_axis=1, co...  97.4 us
    all_to_all x2, waiting for transfers between devices, inverse_columns(): lax.all_to_all(jnp.stack([real_part, imag_part]), 'ctx', split_axis=4, co...  85.6 us
    psum x1, blocking collectives, body(): in_sum = lax.psum(in_terms, ('ctx', 'chan'))  40.9 us
    psum x1, blocking collectives, body(): lax.psum((short_terms, out_terms, decay_terms, skip_terms), 'ctx')  37.3 us
    all_to_all x2, waiting for transfers between devices, forward_spectrum(): lax.all_to_all(signals.reshape((1, signal_count, channels, length)), 'ctx...  26.2 us
    psum x1, waiting for transfers between devices, body(): lax.psum((short_terms, out_terms, decay_terms, skip_terms), 'ctx')  21.3 us
  transfers between devices with their start and end apart: 11, of which 10 were waited for; matrix products, arithmetic and copies ran while one was open for 22% of the time, Pallas kernels for 0%

commit v1 on v0

--- a/solution.py
+++ b/solution.py
@@ -244,7 +244,7 @@
     short_sum, out_sum, decay_sum, skip_sum = lax.psum(
         (short_terms, out_terms, decay_terms, skip_terms), "ctx"
     )
-    in_sum = lax.psum(in_terms, ("ctx", "chan"))
+    in_sum = jnp.sum(lax.all_gather(in_terms, ("ctx", "chan")), axis=0)
     return (
         output,
         grad_inputs[0],

time: 659 us -> 645 us (0.979)
  waiting for transfers between devices: 241 us -> 225 us
    all_gather x0 -> x1, blocking collectives: none -> 43.7 us  [body(): in_sum = jnp.sum(lax.all_gather(in_terms, ('ctx', 'chan')), axis=0)]
    psum x1 -> x0, blocking collectives: 40.9 us -> none  [body(): in_sum = lax.psum(in_terms, ('ctx', 'chan'))]
    psum x1, waiting for transfers between devices: 21.3 us -> 0.01 us  [body(): lax.psum((short_terms, out_terms, decay_terms, skip_terms), 'ctx')]
    all_to_all x2, waiting for transfers between devices: 7.28 us -> 15.6 us  [to_tokens(): lax.all_to_all(columns, 'ctx', split_axis=0, concat_axis=3, tiled=True)]
  transfers between devices with their start and end apart: 11 -> 11, of which waited for: 10 -> 9; matrix products, arithmetic and copies ran while one was open for 22% -> 23% of each run, Pallas kernels for 0% -> 0%
where the time goes in v1:
time: 645 us; the launch traced here: 637 us
  waiting for transfers between devices  225 us (35%)
  matrix products  161 us (25%)
  local copies, waits for them, and re-layouts  82.8 us (13%)
  blocking collectives  79.4 us (12%)
  starting transfers between devices  44.5 us (7%)
  other arithmetic  28.9 us (4%)
  between operations  15.7 us (2%)
    dot_general x40, matrix products, contract(): return jnp.einsum(form, left, right, precision=PRECISE)  156 us
    all_to_all x2, waiting for transfers between devices, forward_spectrum(): lax.all_to_all(jnp.stack([rows_real, rows_imag]), 'ctx', split_axis=1, co...  97.4 us
    all_to_all x2, waiting for transfers between devices, inverse_columns(): lax.all_to_all(jnp.stack([real_part, imag_part]), 'ctx', split_axis=4, co...  85.6 us
    all_gather x1, blocking collectives, body(): in_sum = jnp.sum(lax.all_gather(in_terms, ('ctx', 'chan')), axis=0)  43.7 us
    psum x1, blocking collectives, body(): lax.psum((short_terms, out_terms, decay_terms, skip_terms), 'ctx')  35.7 us
    all_to_all x2, waiting for transfers between devices, forward_spectrum(): lax.all_to_all(signals.reshape((1, signal_count, channels, length)), 'ctx...  26.2 us
    all_to_all x2, waiting for transfers between devices, to_tokens(): lax.all_to_all(columns, 'ctx', split_axis=0, concat_axis=3, tiled=True)  15.6 us
  transfers between devices with their start and end apart: 11, of which 9 were waited for; matrix products, arithmetic and copies ran while one was open for 23% of the time, Pallas kernels for 0%

profile of v1, /device:TPU:0, one launch (start us, length us, event | category | flops | bytes accessed | tf_op | source)
XLA Modules:
  0.0 637.0 jit_solution(16009780104876808809)
XLA Ops:
  11.0 4.8 collective-permute-start
  20.5 6.6 %all-to-all-start.4 = ((f32[1,1,1024,128]{2,1,0,3:T(1,128)}), f32[1,1,1024,128]{2,1,0,3:T(1,128)}, u32[]{:S(2)}, u32[]{:S(2)}) async-start(f32[1,1,1024,128]{2,1,0,3:T(1,128)} %copy.246), calls=%async_computation.4 | async-start | bytes 1048576 | tf_op jit(solution)/shard_map/all_to_all | solution.py:112
  32.8 7.8 %all-to-all-done.4 = f32[1,1,1024,128]{2,1,0,3:T(1,128)} async-done(((f32[1,1,1024,128]{2,1,0,3:T(1,128)}), f32[1,1,1024,128]{2,1,0,3:T(1,128)}, u32[]{:S(2)}, u32[]{:S(2)}) %all-to-all-start.4) | async-done | bytes 524320 | tf_op jit(solution)/shard_map/all_to_all | solution.py:112
  51.2 18.4 %all-to-all-done = f32[1,2,1024,128]{2,1,0,3:T(2,128)} async-done(((f32[1,2,1024,128]{2,1,0,3:T(2,128)}), f32[1,2,1024,128]{2,1,0,3:T(2,128)}, u32[]{:S(2)}, u32[]{:S(2)}) %all-to-all-start) | async-done | bytes 1048608 | tf_op jit(solution)/shard_map/all_to_all | solution.py:112
  86.3 35.7 %all-to-all-done.5 = f32[2,16,1,1024,16]{3,4,2,0,1:T(8,128)} async-done(((f32[2,16,1,1024,16]{3,4,2,0,1:T(8,128)}), f32[2,16,1,1024,16]{3,4,2,0,1:T(8,128)}, u32[]{:S(2)}, u32[]{:S(2)}) %all-to-all-start.5) | async-done | bytes 2097184 | tf_op jit(solution)/shard_map/all_to_all | solution.py:124
  145.3 5.7 subtract_bitcast_fusion.1
  157.5 61.7 %all-to-all-done.1 = f32[2,16,2,1024,16]{3,4,2,0,1:T(8,128)} async-done(((f32[2,16,2,1024,16]{3,4,2,0,1:T(8,128)}), f32[2,16,2,1024,16]{3,4,2,0,1:T(8,128)}, u32[]{:S(2)}, u32[]{:S(2)}) %all-to-all-start.1) | async-done | bytes 4194336 | tf_op jit(solution)/shard_map/all_to_all | solution.py:124
  224.1 7.9 %fusion.26 = f32[2,2,1024,64,2]{2,4,3,1,0:T(2,128)S(1)} fusion(f32[2,2,1024,2,64]{2,4,3,1,0:T(8,128)S(1)} %get-tuple-element.68), kind=kOutput, calls=%fused_computation.48 | convolution fusion | flops 12582968 | bytes 4194304 | tf_op jit(solution)/shard_map/cb,...ba->...ca/dot_general | solution.py:31
  232.0 8.3 %fusion.22 = f32[2,2,1024,64,2]{2,4,3,1,0:T(2,128)S(1)} fusion(f32[2,2,1024,2,64]{2,4,3,1,0:T(8,128)S(1)} %get-tuple-element.69), kind=kOutput, calls=%fused_computation.44 | convolution fusion | flops 12582968 | bytes 4194304 | tf_op jit(solution)/shard_map/cb,...ba->...ca/dot_general | solution.py:31
  240.3 8.2 %convolution_add_fusion = f32[2,2,1024,64,2]{2,4,3,1,0:T(2,128)S(1)} fusion(f32[2,2,1024,64,2]{2,4,3,1,0:T(2,128)S(1)} %fusion.26, f32[2,2,1024,2,64]{2,4,3,1,0:T(8,128)S(1)} %get-tuple-element.69), kind=kOutput, calls=%fused_computation.42 | convolution fusion | flops 13107256 | bytes 6291456 | tf_op jit(solution)/shard_map/cb,...ba->...ca/dot_general | solution.py:31
  248.6 11.2 %fusion.2 = (f32[2,2,1024,2,64]{2,3,4,1,0:T(2,128)S(1)}, f32[2,2,1024,2,64]{2,3,4,1,0:T(2,128)S(1)}) fusion(f32[2,2,1024,64,2]{2,4,3,1,0:T(2,128)S(1)} %convolution_add_fusion, f32[2,64]{0,1:T(8,128)S(1)} %copy-done.20, f32[2,64]{0,1:T(8,128)S(1)} %copy-done.22, f32[2,2,1024,64,2]{2,4,3,1,0:T(2,128)S(1)} %fusion.22, ...), kind=kOutput, calls=%fused_computation.14 | convolution fusion | flops 16252984 | bytes 10486784 | tf_op jit(solution)/shard_map/cb,...ba->...ca/dot_general | solution.py:31
  284.9 9.6 %multiply_subtract_fusion = (f32[2,2,1024,2,64]{2,3,4,1,0:T(2,128)S(1)}, f32[2,2,1024,2,64]{2,3,4,1,0:T(2,128)S(1)}) fusion(f32[2,64]{0,1:T(8,128)S(1)} %copy-done.20, f32[2,64]{0,1:T(8,128)S(1)} %copy-done.22, f32[2,2,1024,2,64]{2,4,3,1,0:T(8,128)S(1)} %fusion.13, f32[2,2,1024,2,64]{2,4,3,1,0:T(8,128)S(1)} %fusion.15, ...), kind=kLoop, calls=%fused_computation.23 | loop fusion | flops 4194304 | bytes 12583936 | tf_op jit(solution)/shard_map/sub | solution.py:39
  294.5 7.5 %fusion.190 = f32[2,2,1024,64,2]{2,4,3,1,0:T(2,128)S(1)} fusion(f32[2,2,1024,2,64]{2,3,4,1,0:T(2,128)S(1)} %get-tuple-element.60), kind=kOutput, calls=%fused_computation.283 | convolution fusion | flops 12582968 | bytes 4194304 | tf_op jit(solution)/shard_map/bc,...ca->...ba/dot_general | solution.py:31
  302.0 7.5 %fusion.188 = f32[2,2,1024,64,2]{2,4,3,1,0:T(2,128)S(1)} fusion(f32[2,2,1024,2,64]{2,3,4,1,0:T(2,128)S(1)} %get-tuple-element.61), kind=kOutput, calls=%fused_computation.281 | convolution fusion | flops 12582968 | bytes 4194304 | tf_op jit(solution)/shard_map/bc,...ca->...ba/dot_general | solution.py:31
  309.6 8.4 %subtract_bitcast_fusion = f32[2,2,1024,2,64]{2,3,4,1,0:T(2,128)S(1)} fusion(f32[2,2,1024,64,2]{2,4,3,1,0:T(2,128)S(1)} %fusion.190, f32[2,2,1024,2,64]{2,3,4,1,0:T(2,128)S(1)} %get-tuple-element.61), kind=kOutput, calls=%fused_computation.21 | convolution fusion | flops 13107256 | bytes 6291456 | tf_op jit(solution)/shard_map/bc,...ca->...ba/dot_general | solution.py:31
  317.9 8.0 %add_bitcast_fusion = f32[2,2,1024,2,64]{2,3,4,1,0:T(2,128)S(1)} fusion(f32[2,2,1024,64,2]{2,4,3,1,0:T(2,128)S(1)} %fusion.188, f32[2,2,1024,2,64]{2,3,4,1,0:T(2,128)S(1)} %get-tuple-element.60), kind=kOutput, calls=%fused_computation.20 | convolution fusion | flops 13107256 | bytes 6291456 | tf_op jit(solution)/shard_map/bc,...ca->...ba/dot_general | solution.py:31
  328.8 5.2 copy.268
  334.0 5.0 all-to-all-start.6
  366.8 64.8 %all-to-all-done.6 = f32[2,2,2,1024,128]{3,2,1,0,4:T(2,128)} async-done(((f32[2,2,2,1024,128]{3,2,1,0,4:T(2,128)}), f32[2,2,2,1024,128]{3,2,1,0,4:T(2,128)}, u32[]{:S(2)}, u32[]{:S(2)}) %all-to-all-start.6) | async-done | bytes 4194336 | tf_op jit(solution)/shard_map/all_to_all | solution.py:149
  462.9 20.8 %all-to-all-done.2 = f32[2,2,1,1024,128]{3,1,2,0,4:T(2,128)} async-done(((f32[2,2,1,1024,128]{3,1,2,0,4:T(2,128)}), f32[2,2,1,1024,128]{3,1,2,0,4:T(2,128)}, u32[]{:S(2)}, u32[]{:S(2)}) %all-to-all-start.2) | async-done | bytes 2097184 | tf_op jit(solution)/shard_map/all_to_all | solution.py:149
  506.5 7.3 %all-to-all-done.7 = f32[8,2,1024,16]{2,3,1,0:T(8,128)} async-done(((f32[8,2,1024,16]{2,3,1,0:T(8,128)}), f32[8,2,1024,16]{2,3,1,0:T(8,128)}, u32[]{:S(2)}, u32[]{:S(2)}) %all-to-all-start.7) | async-done | bytes 1048608 | tf_op jit(solution)/shard_map/all_to_all | solution.py:162
  523.7 8.3 %all-to-all-done.3 = f32[8,1,1024,16]{2,3,1,0:T(8,128)} async-done(((f32[8,1,1024,16]{2,3,1,0:T(8,128)}), f32[8,1,1024,16]{2,3,1,0:T(8,128)}, u32[]{:S(2)}, u32[]{:S(2)}) %all-to-all-start.3) | async-done | bytes 524320 | tf_op jit(solution)/shard_map/all_to_all | solution.py:162
  539.1 35.7 %all-reduce = (f32[3,3,1024]{2,0,1:T(4,128)S(1)}, f32[1024]{0:T(1024)S(1)}, f32[1024]{0:T(1024)S(1)}) all-reduce(f32[3,3,1024]{2,0,1:T(4,128)S(1)} %pad_maximum_fusion.14, f32[1024]{0:T(1024)S(1)} %get-tuple-element.106, f32[1024]{0:T(1024)S(1)} %get-tuple-element.96), channel_id=1, replica_groups=mesh['ctx'=8,'chan'=4] {'ctx'}, use_global_device_ids=true, to_apply=%region_3.4 | all-reduce | flops 11264 | bytes 90112 | tf_op jit(solution)/shard_map/psum | solution.py:244
  577.3 43.7 %all-gather = f32[2048,64]{1,0:T(8,128)S(1)} all-gather(f32[64,64]{1,0:T(8,128)S(1)} %copy-done.23), channel_id=2, replica_groups=mesh['ctx'=8,'chan'=4] {'ctx','chan'}, dimensions={0}, use_global_device_ids=true | all-gather | bytes 540672 | tf_op jit(solution)/shard_map/all_gather | solution.py:247
  (213 shorter events, 213.3 us)
Async XLA Ops:
  7.2 22.2 %copy-start = (f32[64,1024]{1,0:T(8,128)S(1)}, f32[64,1024]{1,0:T(8,128)}, u32[]{:S(2)}) copy-start(f32[64,1024]{1,0:T(8,128)} %param.14) | copy-start | bytes 786436
  8.3 7.5 %copy-start.27 = (f32[3,3,1024]{2,1,0:T(4,128)S(1)}, f32[3,3,1024]{2,1,0:T(4,128)}, u32[]{:S(2)}) copy-start(f32[3,3,1024]{2,1,0:T(4,128)} %param.12) | copy-start | bytes 110596
  8.3 7.7 %copy-start.36 = (f32[1024]{0:T(1024)S(1)}, f32[1024]{0:T(1024)}, u32[]{:S(2)}) copy-start(f32[1024]{0:T(1024)} %param.15) | copy-start | bytes 12292
  8.4 7.8 %copy-start.18 = (bf16[1024,128]{1,0:T(8,128)(2,1)S(1)}, bf16[1024,128]{1,0:T(8,128)(2,1)}, u32[]{:S(2)}) copy-start(bf16[1024,128]{1,0:T(8,128)(2,1)} %param.17) | copy-start | bytes 786436
  9.6 7.4 %copy-start.10 = (bf16[1024,128]{0,1:T(8,128)(2,1)}, bf16[1024,128]{0,1:T(8,128)(2,1)S(1)}, u32[]{:S(2)}) copy-start(bf16[1024,128]{0,1:T(8,128)(2,1)S(1)} %copy.215) | copy-start | bytes 786436
  10.8 6.5 %copy-start.11 = (bf16[1024,128]{0,1:T(8,128)(2,1)}, bf16[1024,128]{0,1:T(8,128)(2,1)S(1)}, u32[]{:S(2)}) copy-start(bf16[1024,128]{0,1:T(8,128)(2,1)S(1)} %copy.216) | copy-start | bytes 786436
  11.0 6.2 collective-permute-start
  20.5 20.0 %all-to-all-start.4 = ((f32[1,1,1024,128]{2,1,0,3:T(1,128)}), f32[1,1,1024,128]{2,1,0,3:T(1,128)}, u32[]{:S(2)}, u32[]{:S(2)}) async-start(f32[1,1,1024,128]{2,1,0,3:T(1,128)} %copy.246), calls=%async_computation.4 | async-start | bytes 1048576 | tf_op jit(solution)/shard_map/all_to_all | solution.py:112
  40.6 29.0 %all-to-all-start = ((f32[1,2,1024,128]{2,1,0,3:T(2,128)}), f32[1,2,1024,128]{2,1,0,3:T(2,128)}, u32[]{:S(2)}, u32[]{:S(2)}) async-start(f32[1,2,1024,128]{2,1,0,3:T(2,128)} %copy.217), calls=%async_computation | async-start | bytes 2097152 | tf_op jit(solution)/shard_map/all_to_all | solution.py:112
  69.6 52.4 %all-to-all-start.5 = ((f32[2,16,1,1024,16]{3,4,2,0,1:T(8,128)}), f32[2,16,1,1024,16]{3,4,2,0,1:T(8,128)}, u32[]{:S(2)}, u32[]{:S(2)}) async-start(f32[2,16,1,1024,16]{3,4,2,0,1:T(8,128)} %copy.248), calls=%async_computation.5 | async-start | bytes 4194304 | tf_op jit(solution)/shard_map/all_to_all | solution.py:124
  122.0 97.3 %all-to-all-start.1 = ((f32[2,16,2,1024,16]{3,4,2,0,1:T(8,128)}), f32[2,16,2,1024,16]{3,4,2,0,1:T(8,128)}, u32[]{:S(2)}, u32[]{:S(2)}) async-start(f32[2,16,2,1024,16]{3,4,2,0,1:T(8,128)} %copy.220), calls=%async_computation.1 | async-start | bytes 8388608 | tf_op jit(solution)/shard_map/all_to_all | solution.py:124
  141.2 4.1 copy-start.19
  141.2 4.1 copy-start.21
  240.3 8.3 %copy-start.20 = (f32[2,64]{0,1:T(8,128)S(1)}, f32[2,64]{0,1:T(8,128)}, u32[]{:S(2)}) copy-start(f32[2,64]{0,1:T(8,128)} %copy.229) | copy-start | bytes 1540
  240.3 8.3 %copy-start.22 = (f32[2,64]{0,1:T(8,128)S(1)}, f32[2,64]{0,1:T(8,128)}, u32[]{:S(2)}) copy-start(f32[2,64]{0,1:T(8,128)} %copy.226) | copy-start | bytes 1540
  334.0 97.5 %all-to-all-start.6 = ((f32[2,2,2,1024,128]{3,2,1,0,4:T(2,128)}), f32[2,2,2,1024,128]{3,2,1,0,4:T(2,128)}, u32[]{:S(2)}, u32[]{:S(2)}) async-start(f32[2,2,2,1024,128]{3,2,1,0,4:T(2,128)} %copy.268), calls=%async_computation.6 | async-start | bytes 8388608 | tf_op jit(solution)/shard_map/all_to_all | solution.py:149
  358.5 4.7 copy-start.35
  431.5 52.2 %all-to-all-start.2 = ((f32[2,2,1,1024,128]{3,1,2,0,4:T(2,128)}), f32[2,2,1,1024,128]{3,1,2,0,4:T(2,128)}, u32[]{:S(2)}, u32[]{:S(2)}) async-start(f32[2,2,1,1024,128]{3,1,2,0,4:T(2,128)} %copy.240), calls=%async_computation.2 | async-start | bytes 4194304 | tf_op jit(solution)/shard_map/all_to_all | solution.py:149
  483.7 30.1 %all-to-all-start.7 = ((f32[8,2,1024,16]{2,3,1,0:T(8,128)}), f32[8,2,1024,16]{2,3,1,0:T(8,128)}, u32[]{:S(2)}, u32[]{:S(2)}) async-start(f32[8,2,1024,16]{2,3,1,0:T(8,128)} %copy.272), calls=%async_computation.7 | async-start | bytes 2097152 | tf_op jit(solution)/shard_map/all_to_all | solution.py:162
  513.8 18.2 %all-to-all-start.3 = ((f32[8,1,1024,16]{2,3,1,0:T(8,128)}), f32[8,1,1024,16]{2,3,1,0:T(8,128)}, u32[]{:S(2)}, u32[]{:S(2)}) async-start(f32[8,1,1024,16]{2,3,1,0:T(8,128)} %copy.244), calls=%async_computation.3 | async-start | bytes 1048576 | tf_op jit(solution)/shard_map/all_to_all | solution.py:162
  517.9 110.2 %all-reduce.3.cloned.1.call-start = ((), (), s32[]{:S(2)}) async-start(), calls=%async_computation.8 | async-start | bytes 524288 | tf_op jit(solution)/shard_map/psum | solution.py:244
  532.0 4.7 copy-start.26
  536.7 40.6 %copy-start.23 = (f32[64,64]{1,0:T(8,128)S(1)}, f32[64,64]{1,0:T(8,128)}, u32[]{:S(2)}) copy-start(f32[64,64]{1,0:T(8,128)} %fusion.105) | copy-start | bytes 49156
  576.0 47.4 %collective-permute-start.1 = (f32[3,1024,2]{1,2,0:T(2,128)}, f32[3,1024,2]{1,2,0:T(2,128)}, u32[]{:S(2)}, u32[]{:S(2)}) collective-permute-start(f32[3,1024,2]{1,2,0:T(2,128)} %slice.161), channel_id=1, source_target_pairs={{4,0},{8,4},{12,8},{16,12},{20,16},{24,20},{28,24},{5,1},{9,5},{13... | collective-permute-start | bytes 73736 | tf_op jit(solution)/shard_map/ppermute | solution.py:13
  (25 other events, 52.7 us)
Sparse Core Ops, SparseCore 0:
  536.8 70.1 all-reduce.2
